TPU v7x, 128 devices: a whole 4x4x4 slice. The times are simulated.
128 devices in a mesh: stream: 64 (over z, y, x), seq: 2 (over core).
Axes of the slice: x: 4, y: 4, z: 4, core: 2. Of those that a mesh axis runs over, the one named last changes fastest.
Arguments:
- head_inputs: bfloat16 [64, 3072, 1536], P('stream', 'seq'), may hold values from -6 to 6
- state_maps: bfloat16 [64, 3072, 256], P('stream', 'seq'), may hold values from -2.1 to 2.1
- step_logits: float32 [64, 24, 3072], P('stream', None, 'seq'), may hold values from -3 to 5.5
- log_rates: float32 [24], replicated, may hold values from -7 to 0
- step_bias: float32 [24], replicated, may hold values from -6 to -2
- skip_gain: float32 [24], replicated, may hold values from 0.25 to 1.75
- old_states: float32 [64, 24, 64, 128], P('stream', 'seq'), may hold values from -6 to 6
- old_owner: int32 [64], replicated, may hold values from 0 to 63, as said below
- doc_starts: int32 [64, 2], P('stream'), may hold values from 0 to 3071
- grad_output: bfloat16 [64, 3072, 1536], P('stream', 'seq'), may hold values from -6 to 6
Outputs:
- layer_out: bfloat16 [64, 3072, 1536], P('stream', 'seq')
- grad_inputs: bfloat16 [64, 3072, 1536], P('stream', 'seq')
- grad_maps: bfloat16 [64, 3072, 256], P('stream', 'seq')
- grad_logits: float32 [64, 24, 3072], P('stream', None, 'seq')
- grad_rates: float32 [24], replicated
- grad_bias: float32 [24], replicated
- grad_skip: float32 [24], replicated
Inputs may be any that keep to these rules, and one draw needn't show every extreme that they name: A permutation of the 64 stream indices: new stream s continues old stream old_owner[s]. `doc_starts`: positions in a stream's segment where a document starts and the state is cleared; entries may repeat.
All inputs are finite; a program needn't handle non-finite values.
Results may differ from a plain program's by a relative error of at most 0.013.
Values sent between devices are 32-bit elements; how exact they have to be, the bound alone decides.
No kernel may reach another device: no remote copies, remote signals or barrier semaphores. Data moves between devices by JAX's collectives and lax.ppermute only.
A program may use at most 192 MiB of HBM per device.

v0:
```python
import jax
import jax.numpy as jnp
from jax import lax
from jax.sharding import PartitionSpec as P

GROUP = 256


def shifted_2(shard, axis, by):
    size = lax.axis_size(axis)
    pairs = [(i, i + by) for i in range(size) if 0 <= i + by < size]
    return lax.ppermute(shard, axis, pairs)


def decay_terms(logits_part, flags_part, log_rates, step_bias):
    step_size = jax.nn.softplus(logits_part + step_bias[:, None])
    cum_decay = jnp.cumsum(-step_size * jnp.exp(log_rates)[:, None], axis=-1)
    doc_index = jnp.cumsum(flags_part, axis=-1)
    return (step_size, cum_decay, doc_index)


def group_states(inputs_c, maps_c, logits_c, flags_c, log_rates, step_bias):
    step_size, cum_decay, doc_index = decay_terms(logits_c, flags_c, log_rates, step_bias)
    state_n = maps_c.shape[-1] // 2
    b_part = maps_c[:, :, :state_n].astype(jnp.float32)
    same_doc = doc_index == doc_index[:, -1:]
    weight = (
        jnp.where(same_doc[:, None, :], jnp.exp(cum_decay[:, :, -1:] - cum_decay), 0.0) * step_size
    )
    b_weighted = (weight[:, :, :, None] * b_part[:, None, :, :]).astype(jnp.bfloat16)
    states = jnp.einsum("cjhp,chjn->chpn", inputs_c, b_weighted, preferred_element_type=jnp.float32)
    decays = jnp.where(doc_index[:, -1:] == 0, jnp.exp(cum_decay[:, :, -1]), 0.0)
    return (states, decays)


def group_inputs(start_state, states, decays):

    def advance(carry, members):
        group_state, group_decay = members
        return (group_decay[:, None, None] * carry + group_state, carry)

    return lax.scan(advance, start_state, (states, decays))


def one_group(inputs_q, maps_q, logits_q, flags_q, starts_q, log_rates, step_bias, skip_gain):
    step_size, cum_decay, doc_index = decay_terms(logits_q, flags_q, log_rates, step_bias)
    state_n = maps_q.shape[-1] // 2
    b_part = maps_q[:, :state_n]
    c_part = maps_q[:, state_n:]
    scores = jnp.dot(c_part, b_part.T, preferred_element_type=jnp.float32)
    position = jnp.arange(maps_q.shape[0])
    visible = (position[None, :] <= position[:, None]) & (doc_index[None, :] == doc_index[:, None])
    log_gaps = jnp.where(visible[None], cum_decay[:, :, None] - cum_decay[:, None, :], -jnp.inf)
    mixing = (scores[None] * jnp.exp(log_gaps) * step_size[:, None, :]).astype(jnp.bfloat16)
    local_part = jnp.einsum("hij,jhp->ihp", mixing, inputs_q, preferred_element_type=jnp.float32)
    inflow = jnp.where(doc_index[None, :] == 0, jnp.exp(cum_decay), 0.0)
    carried = jnp.einsum(
        "in,hpn->ihp", c_part.astype(jnp.float32), starts_q, precision=lax.Precision.HIGHEST
    )
    summed = (
        local_part
        + carried * inflow.T[:, :, None]
        + skip_gain[None, :, None] * inputs_q.astype(jnp.float32)
    )
    return summed.reshape(inputs_q.shape[0], -1).astype(jnp.bfloat16)


def outputs(inputs_c, maps_c, logits_c, flags_c, log_rates, step_bias, skip_gain, starts_c):

    def per_group(carry, members):
        inputs_q, maps_q, logits_q, flags_q, starts_q = members
        return (
            carry,
            jax.checkpoint(one_group)(
                inputs_q, maps_q, logits_q, flags_q, starts_q, log_rates, step_bias, skip_gain
            ),
        )

    _, result = lax.scan(per_group, 0, (inputs_c, maps_c, logits_c, flags_c, starts_c))
    return result


def shards(
    head_inputs,
    state_maps,
    step_logits,
    log_rates,
    step_bias,
    skip_gain,
    old_states,
    old_owner,
    doc_starts,
    grad_output,
):
    length = head_inputs.shape[1]
    head_count = step_logits.shape[1]
    head_dim = old_states.shape[2]
    state_n = old_states.shape[3]
    groups = length // GROUP
    seq_index = lax.axis_index("seq")
    stream_index = lax.axis_index("stream")
    position = seq_index * length + lax.iota(jnp.int32, length)
    reset_flags = jnp.any(doc_starts[0][:, None] == position[None, :], axis=0).astype(jnp.int32)
    gathered = lax.all_gather(old_states, "stream", axis=0, tiled=True)
    own_block = lax.dynamic_index_in_dim(gathered, old_owner[stream_index], 0, keepdims=False)
    start_state = lax.all_gather(own_block, "seq", axis=0, tiled=True)
    inputs_c = head_inputs[0].reshape(groups, GROUP, head_count, head_dim)
    maps_c = state_maps[0].reshape(groups, GROUP, 2 * state_n)
    logits_c = step_logits[0].reshape(head_count, groups, GROUP).transpose(1, 0, 2)
    flags_c = reset_flags.reshape(groups, GROUP)

    def state_part(inputs_c, maps_c, logits_c, log_rates, step_bias):
        return group_states(inputs_c, maps_c, logits_c, flags_c, log_rates, step_bias)

    (states, decays), pull_states = jax.vjp(
        state_part, inputs_c, maps_c, logits_c, log_rates, step_bias
    )
    empty_state = jnp.zeros((head_count, head_dim, state_n), jnp.float32)
    local_state, _ = group_inputs(empty_state, states, decays)
    shard_decay = jnp.prod(decays, axis=0)
    is_first = seq_index == 0

    def forward_turn(counter, entering):
        leaving = shard_decay[:, None, None] * entering + local_state
        shifted = shifted_2(leaving, "seq", 1)
        return jnp.where(is_first, start_state, shifted)

    entry_state = lax.fori_loop(0, lax.axis_size("seq") - 1, forward_turn, start_state)
    (exit_state, starts_c), pull_inputs = jax.vjp(group_inputs, entry_state, states, decays)

    def output_part(inputs_c, maps_c, logits_c, log_rates, step_bias, skip_gain, starts_c):
        return outputs(
            inputs_c, maps_c, logits_c, flags_c, log_rates, step_bias, skip_gain, starts_c
        )

    result, pull_output = jax.vjp(
        output_part, inputs_c, maps_c, logits_c, log_rates, step_bias, skip_gain, starts_c
    )
    grads_c = grad_output[0].reshape(groups, GROUP, head_count * head_dim)
    in_first, maps_first, logits_first, rates_first, bias_first, skip_total, grad_starts = (
        pull_output(grads_c)
    )
    from_output = pull_inputs((jnp.zeros_like(exit_state), grad_starts))[0]

    def backward_turn(counter, leaving_grad):
        entering_grad = shard_decay[:, None, None] * leaving_grad + from_output
        return shifted_2(entering_grad, "seq", -1)

    exit_grad = lax.fori_loop(0, lax.axis_size("seq") - 1, backward_turn, empty_state)
    _, grad_states, grad_decays = pull_inputs((exit_grad, grad_starts))
    in_second, maps_second, logits_second, rates_second, bias_second = pull_states(
        (grad_states, grad_decays)
    )
    rates_total, bias_total, skip_sum = lax.psum(
        (rates_first + rates_second, bias_first + bias_second, skip_total), ("stream", "seq")
    )
    grad_logits = (logits_first + logits_second).transpose(1, 0, 2).reshape(1, head_count, length)
    return (
        result.reshape(1, length, -1),
        (in_first + in_second).reshape(1, length, -1),
        (maps_first + maps_second).reshape(1, length, -1),
        grad_logits,
        rates_total,
        bias_total,
        skip_sum,
    )


def solution(mesh):
    return jax.shard_map(
        shards,
        mesh=mesh,
        in_specs=(
            P("stream", "seq", None),
            P("stream", "seq", None),
            P("stream", None, "seq"),
            P(),
            P(),
            P(),
            P("stream", "seq", None, None),
            P(),
            P("stream", None),
            P("stream", "seq", None),
        ),
        out_specs=(
            P("stream", "seq", None),
            P("stream", "seq", None),
            P("stream", "seq", None),
            P("stream", None, "seq"),
            P(),
            P(),
            P(),
        ),
        check_vma=False,
    )
```

profile of v0, /device:TPU:1, one launch (start us, length us, event | category | flops | bytes accessed | tf_op | source)
XLA Modules:
  0.0 601.4 jit_solution(6530939128043399756)
XLA Ops:
  21.2 12.9 %reshape.634 = bf16[6,256,24,64]{3,2,1,0:T(8,128)(2,1)} reshape(bf16[1,1536,1536]{2,1,0:T(8,128)(2,1)} %param.22) | data formatting | bytes 9437184 | tf_op jit(solution)/shard_map/reshape;squeeze | solution.py:107
  34.1 10.3 %copy.231 = bf16[6,256,24,64]{1,3,2,0:T(8,128)(2,1)} copy(bf16[6,256,24,64]{3,2,1,0:T(8,128)(2,1)} %reshape.634) | data formatting | bytes 9437184
  46.2 8.0 %fusion.94 = f32[6,24,64,128]{3,2,1,0:T(8,128)} fusion(bf16[6,256,24,64]{1,3,2,0:T(8,128)(2,1)} %copy.231, f32[6,256,128]{1,2,0:T(8,128)S(1)} %copy.228, f32[6,24,256]{2,1,0:T(8,128)S(1)} %select_multiply_fusion.3), kind=kOutput, calls=%fused_computation.172 | convolution fusion | flops 613416960 | bytes 10371072 | tf_op jit(solution)/shard_map/jvp(cjhp,chjn->chpn)/dot_general | solution.py:31
  54.2 8.2 %while.108 = (s32[]{:T(128)}, f32[24,64,128]{2,1,0:T(8,128)S(1)}, f32[6,24]{1,0:T(8,128)S(1)}, f32[6,24,64,128]{3,2,1,0:T(8,128)}, s32[]{:T(128)}, /*index=5*/s32[]{:T(128)}) while((s32[]{:T(128)}, f32[24,64,128]{2,1,0:T(8,128)S(1)}, f32[6,24]{1,0:T(8,128)S(1)}, f32[6,24,64,128]{3,2,1,0:T(8,128)}, s32[]{:T(128)}, ...), condition=%wide.region_7.8_spmd.clone, body=%wide.region_6.7_spmd.clone.sunk | while | flops 589827 | bytes 2359671 | solution.py:42
  62.4 83.2 %all-gather.3.cloned.1.call-done = f32[64,12,64,128]{3,2,1,0:T(8,128)} async-done(((f32[1,12,64,128]{3,2,1,0:T(8,128)}), f32[64,12,64,128]{3,2,1,0:T(8,128)}) %all-gather.3.cloned.1.call-update) | async-done | bytes 25165840 | tf_op jit(solution)/shard_map/all_gather | solution.py:104
  157.7 17.0 %while.105 = (s32[]{:T(128)}, f32[24,64,128]{2,1,0:T(8,128)S(1)}, f32[6,24,64,128]{3,2,1,0:T(8,128)}, f32[6,24,1,1]{1,3,2,0:T(1,128)}, f32[6,24]{1,0:T(8,128)S(1)}, /*index=5*/f32[6,24,64,128]{3,2,1,0:T(8,128)}, s32[]{:T(128)}) while((s32[]{:T(128)}, f32[24,64,128]{2,1,0:T(8,128)S(1)}, f32[6,24,64,128]{3,2,1,0:T(8,128)}, ...), condition=%wide.region_9.10_spmd, body=%wide.region_8.9_spmd.sunk | while | flops 393218 | bytes 3934165 | solution.py:42
  181.7 195.7 %while.109 = (s32[]{:T(128)}, f32[24]{0:T(128)}, f32[24]{0:T(128)}, f32[24]{0:T(128)}, bf16[6,256,24,64]{1,3,2,0:T(8,128)(2,1)}, /*index=5*/bf16[6,256,256]{1,2,...) while((s32[]{:T(128)}, f32[24]{0:T(128)}, f32[24]{0:T(128)}, ...), condition=%wide.region_31.32_spmd.clone, body=%wide.region_16.31_spmd.clone.sunk | while | flops 2306163200 | bytes 22004424 | solution.py:79
  193.2 6.2 %fusion.183 = (f32[24,256]{1,0:T(8,128)S(1)}, f32[24,256]{1,0:T(8,128)S(1)}, f32[24,256]{1,0:T(8,128)}, bf16[256,256]{1,0:T(8,128)(2,1)S(1)}) fusion(f32[24,256]{1,0:T(8,128)S(1)} %copy_bitcast_fusion.13, f32[24,256]{1,0:T(8,128)} %get-tuple-element.1559, f32[256,256]{1,0:T(8,128)S(1)} %fusion.181, pred[256,256]{1,0:T(8,128)(4,1)S(1)} %fusion.182, ...), kind=kOutput, calls=%fused_computation.73.clone.1 | convolution fusion | flops 224835584 | bytes 2154496 | tf_op jit(solution)/shard_map/transpose(jvp())/while/body/eval_jaxpr/checkpoint/hij,jhp->ihp/dot_general | solution.py:55
  225.8 6.2 %fusion.183 = (f32[24,256]{1,0:T(8,128)S(1)}, f32[24,256]{1,0:T(8,128)S(1)}, f32[24,256]{1,0:T(8,128)}, bf16[256,256]{1,0:T(8,128)(2,1)S(1)}) fusion(f32[24,256]{1,0:T(8,128)S(1)} %copy_bitcast_fusion.13, f32[24,256]{1,0:T(8,128)} %get-tuple-element.1559, f32[256,256]{1,0:T(8,128)S(1)} %fusion.181, pred[256,256]{1,0:T(8,128)(4,1)S(1)} %fusion.182, ...), kind=kOutput, calls=%fused_computation.73.clone.1 | convolution fusion | flops 224835584 | bytes 2154496 | tf_op jit(solution)/shard_map/transpose(jvp())/while/body/eval_jaxpr/checkpoint/hij,jhp->ihp/dot_general | solution.py:55
  258.4 6.2 %fusion.183 = (f32[24,256]{1,0:T(8,128)S(1)}, f32[24,256]{1,0:T(8,128)S(1)}, f32[24,256]{1,0:T(8,128)}, bf16[256,256]{1,0:T(8,128)(2,1)S(1)}) fusion(f32[24,256]{1,0:T(8,128)S(1)} %copy_bitcast_fusion.13, f32[24,256]{1,0:T(8,128)} %get-tuple-element.1559, f32[256,256]{1,0:T(8,128)S(1)} %fusion.181, pred[256,256]{1,0:T(8,128)(4,1)S(1)} %fusion.182, ...), kind=kOutput, calls=%fused_computation.73.clone.1 | convolution fusion | flops 224835584 | bytes 2154496 | tf_op jit(solution)/shard_map/transpose(jvp())/while/body/eval_jaxpr/checkpoint/hij,jhp->ihp/dot_general | solution.py:55
  270.4 3.9 fusion.189
  291.0 6.2 %fusion.183 = (f32[24,256]{1,0:T(8,128)S(1)}, f32[24,256]{1,0:T(8,128)S(1)}, f32[24,256]{1,0:T(8,128)}, bf16[256,256]{1,0:T(8,128)(2,1)S(1)}) fusion(f32[24,256]{1,0:T(8,128)S(1)} %copy_bitcast_fusion.13, f32[24,256]{1,0:T(8,128)} %get-tuple-element.1559, f32[256,256]{1,0:T(8,128)S(1)} %fusion.181, pred[256,256]{1,0:T(8,128)(4,1)S(1)} %fusion.182, ...), kind=kOutput, calls=%fused_computation.73.clone.1 | convolution fusion | flops 224835584 | bytes 2154496 | tf_op jit(solution)/shard_map/transpose(jvp())/while/body/eval_jaxpr/checkpoint/hij,jhp->ihp/dot_general | solution.py:55
  323.7 6.2 %fusion.183 = (f32[24,256]{1,0:T(8,128)S(1)}, f32[24,256]{1,0:T(8,128)S(1)}, f32[24,256]{1,0:T(8,128)}, bf16[256,256]{1,0:T(8,128)(2,1)S(1)}) fusion(f32[24,256]{1,0:T(8,128)S(1)} %copy_bitcast_fusion.13, f32[24,256]{1,0:T(8,128)} %get-tuple-element.1559, f32[256,256]{1,0:T(8,128)S(1)} %fusion.181, pred[256,256]{1,0:T(8,128)(4,1)S(1)} %fusion.182, ...), kind=kOutput, calls=%fused_computation.73.clone.1 | convolution fusion | flops 224835584 | bytes 2154496 | tf_op jit(solution)/shard_map/transpose(jvp())/while/body/eval_jaxpr/checkpoint/hij,jhp->ihp/dot_general | solution.py:55
  356.3 6.2 %fusion.183 = (f32[24,256]{1,0:T(8,128)S(1)}, f32[24,256]{1,0:T(8,128)S(1)}, f32[24,256]{1,0:T(8,128)}, bf16[256,256]{1,0:T(8,128)(2,1)S(1)}) fusion(f32[24,256]{1,0:T(8,128)S(1)} %copy_bitcast_fusion.13, f32[24,256]{1,0:T(8,128)} %get-tuple-element.1559, f32[256,256]{1,0:T(8,128)S(1)} %fusion.181, pred[256,256]{1,0:T(8,128)(4,1)S(1)} %fusion.182, ...), kind=kOutput, calls=%fused_computation.73.clone.1 | convolution fusion | flops 224835584 | bytes 2154496 | tf_op jit(solution)/shard_map/transpose(jvp())/while/body/eval_jaxpr/checkpoint/hij,jhp->ihp/dot_general | solution.py:55
  368.3 3.9 fusion.189
  377.5 11.6 %while.110 = (s32[]{:T(128)}, f32[24,64,128]{2,1,0:T(8,128)S(1)}, f32[6,24,64,128]{3,2,1,0:T(8,128)}, f32[6,24,1,1]{1,3,2,0:T(1,128)}, s32[]{:T(128)}, /*index=5*/s32[]{:T(128)}, s32[]{:T(128)}) while((s32[]{:T(128)}, f32[24,64,128]{2,1,0:T(8,128)S(1)}, f32[6,24,64,128]{3,2,1,0:T(8,128)}, f32[6,24,1,1]{1,3,2,0:T(1,128)}, ...), condition=%wide.region_33.34_spmd.clone, body=%wide.region_32.33_spmd.clone.sunk | while | flops 589828 | bytes 2359691 | solution.py:42
  394.3 15.2 %while.106 = (s32[]{:T(128)}, f32[24,64,128]{2,1,0:T(8,128)S(1)}, bf16[6,24,64,128]{3,2,1,0:T(8,128)(2,1)S(1)}, f32[6,24]{1,0:T(8,128)S(1)}, f32[6,24,64,128]{3,...) while((s32[]{:T(128)}, f32[24,64,128]{2,1,0:T(8,128)S(1)}, ...), condition=%wide.region_36.37_spmd, body=%wide.region_34.36_spmd.sunk | while | flops 786411 | bytes 4719297 | solution.py:42
  410.9 7.1 %fusion.87 = (f32[6,24,256]{2,1,0:T(8,128)S(1)}, bf16[6,256,128]{1,2,0:T(8,128)(2,1)S(1)}) fusion(f32[6,256,128]{1,2,0:T(8,128)} %copy-done.6, f32[6,24,256]{2,1,0:T(8,128)S(1)} %copy-done.16, bf16[6,24,64,128]{3,2,1,0:T(8,128)(2,1)} %copy-done.4, bf16[6,256,24,64]{1,3,2,0:T(8,128)(2,1)} %get-tuple-element.1777), kind=kOutput, calls=%fused_computation.162 | convolution fusion | flops 627339264 | bytes 8552448 | tf_op jit(solution)/shard_map/transpose(jvp(cjhp,chjn->chpn))/dot_general | solution.py:31
  418.8 14.9 %reduce-window.130 = f32[6,24,2,128]{3,1,2,0:T(8,128)S(1)} reduce-window(f32[6,24,2,128]{3,1,2,0:T(8,128)S(1)} %copy_bitcast_fusion.5, f32[]{:T(128)} %constant.289.clone.1), window={size=1x1x1x128 pad=0_0x0_0x0_0x0_127}, to_apply=%region_40.41 | reduce-window | flops 4681728 | bytes 294916 | tf_op jit(solution)/shard_map/reduce-window.14
  436.3 6.9 %bitcast_add_fusion.6 = bf16[6,256,24,64]{1,3,2,0:T(8,128)(2,1)} fusion(bf16[6,256,24,64]{1,3,2,0:T(8,128)(2,1)} %get-tuple-element.766, bf16[6,24,64,128]{3,2,1,0:T(8,128)(2,1)} %copy-done.4, f32[6,256,128]{1,2,0:T(8,128)S(1)} %copy-done.7, f32[6,24,256]{2,1,0:T(8,128)S(1)} %copy-done.16), kind=kOutput, calls=%fused_computation.171 | convolution fusion | flops 615776256 | bytes 12730368 | tf_op jit(solution)/shard_map/transpose(jvp(cjhp,chjn->chpn))/dot_general | solution.py:31
  443.2 10.4 %copy.250 = bf16[6,256,24,64]{3,2,1,0:T(8,128)(2,1)} copy(bf16[6,256,24,64]{1,3,2,0:T(8,128)(2,1)} %bitcast_add_fusion.6) | data formatting | bytes 9437184
  453.6 13.1 %reshape.633 = bf16[1,1536,1536]{2,1,0:T(8,128)(2,1)} reshape(bf16[6,256,24,64]{3,2,1,0:T(8,128)(2,1)} %copy.250) | data formatting | bytes 9437184
  467.4 62.6 %while.107 = (s32[]{:T(128)}, bf16[6,256,1536]{2,1,0:T(8,128)(2,1)}, bf16[6,256,24,64]{1,3,2,0:T(8,128)(2,1)}, bf16[6,256,256]{2,1,0:T(8,128)(2,1)}, s32[6,256]{...) while((s32[]{:T(128)}, bf16[6,256,1536]{2,1,0:T(8,128)(2,1)}, ...), condition=%wide.region_15.16_spmd.clone, body=%wide.region_10.15_spmd.clone.sunk | while | flops 833433920 | bytes 10981461 | solution.py:79
  530.0 64.5 %all-reduce.5 = (f32[24]{0:T(128)}, f32[24]{0:T(128)}, f32[24]{0:T(128)}) all-reduce(f32[24]{0:T(128)S(1)} %get-tuple-element.1226, f32[24]{0:T(128)S(1)} %add.228, f32[24]{0:T(128)S(1)} %copy-done.26), channel_id=1, replica_groups=mesh['stream'=64,'seq'=2] {'stream','seq'}, use_global_device_ids=true, to_apply=%region_43.44 | all-reduce | flops 72 | bytes 576 | tf_op jit(solution)/shard_map/psum | solution.py:154
  (717 shorter events, 306.4 us)
Async XLA Ops:
  7.2 138.5 %all-gather.3.cloned.1.call-start = ((), (), s32[]{:S(2)}) async-start(), calls=%async_computation | async-start | bytes 25559040 | tf_op jit(solution)/shard_map/all_gather | solution.py:104
  14.3 19.8 %copy-start.32 = (f32[24]{0:T(128)}, f32[24]{0:T(128)S(1)}, u32[]{:S(2)}) copy-start(f32[24]{0:T(128)S(1)} %exp.90) | copy-start | bytes 292
  16.1 29.9 %copy-start.1 = (f32[6,24,256]{2,1,0:T(8,128)}, f32[6,24,256]{2,1,0:T(8,128)S(1)}, u32[]{:S(2)}) copy-start(f32[6,24,256]{2,1,0:T(8,128)S(1)} %get-tuple-element.1738) | copy-start | bytes 442372
  19.9 26.1 %copy-start.11 = (f32[6,24,2]{1,2,0:T(2,128)}, f32[6,24,2]{1,2,0:T(2,128)S(1)}, u32[]{:S(2)}) copy-start(f32[6,24,2]{1,2,0:T(2,128)S(1)} %slice.164) | copy-start | bytes 3460
  21.2 25.0 %copy-start.6 = (f32[6,256,128]{1,2,0:T(8,128)}, f32[6,256,128]{1,2,0:T(8,128)S(1)}, u32[]{:S(2)}) copy-start(f32[6,256,128]{1,2,0:T(8,128)S(1)} %copy.228) | copy-start | bytes 2359300
  34.1 11.9 %copy-start.10 = (f32[24]{0:T(128)S(1)}, f32[24]{0:T(128)}, u32[]{:S(2)}) copy-start(f32[24]{0:T(128)} %param.26) | copy-start | bytes 292
  45.3 8.9 %copy-start.13 = (f32[6,24]{1,0:T(8,128)}, f32[6,24]{1,0:T(8,128)S(1)}, u32[]{:S(2)}) copy-start(f32[6,24]{1,0:T(8,128)S(1)} %slice_reduce_fusion.7) | copy-start | bytes 1732
  46.0 8.2 %copy-start.19 = (pred[6,256]{1,0:T(8,128)(4,1)}, pred[6,256]{1,0:T(8,128)(4,1)S(1)}, u32[]{:S(2)}) copy-start(pred[6,256]{1,0:T(8,128)(4,1)S(1)} %broadcast_compare_fusion.2) | copy-start | bytes 4612
  150.3 4.4 collective-permute-start
  270.4 8.0 %copy-start.27 = (f32[24]{0:T(128)S(1)}, f32[24]{0:T(128)}, u32[]{:S(2)}) copy-start(f32[24]{0:T(128)} %get-tuple-element.1642) | copy-start | bytes 292 | tf_op jit(solution)/shard_map/transpose(jvp())/while
  368.3 8.0 %copy-start.27 = (f32[24]{0:T(128)S(1)}, f32[24]{0:T(128)}, u32[]{:S(2)}) copy-start(f32[24]{0:T(128)} %get-tuple-element.1642) | copy-start | bytes 292 | tf_op jit(solution)/shard_map/transpose(jvp())/while
  377.5 11.6 %copy-start.34 = (f32[24]{0:T(128)S(1)}, f32[24]{0:T(128)}, u32[]{:S(2)}) copy-start(f32[24]{0:T(128)} %broadcast_multiply_fusion) | copy-start | bytes 292
  390.1 4.1 collective-permute-start.1
  394.2 15.2 %copy-start.14 = (f32[6,24]{1,0:T(8,128)S(1)}, f32[6,24]{1,0:T(8,128)}, u32[]{:S(2)}) copy-start(f32[6,24]{1,0:T(8,128)} %copy-done.13) | copy-start | bytes 1732
  394.2 15.2 %copy-start.31 = (pred[6]{0:T(512)(128)(4,1)S(1)}, pred[6]{0:T(512)(128)(4,1)}, u32[]{:S(2)}) copy-start(pred[6]{0:T(512)(128)(4,1)} %copy-done.30) | copy-start | bytes 22
  394.2 16.6 %copy-start.16 = (f32[6,24,256]{2,1,0:T(8,128)S(1)}, f32[6,24,256]{2,1,0:T(8,128)}, u32[]{:S(2)}) copy-start(f32[6,24,256]{2,1,0:T(8,128)} %copy-done.15) | copy-start | bytes 442372
  410.9 23.0 %copy-start.33 = (f32[24]{0:T(128)S(1)}, f32[24]{0:T(128)}, u32[]{:S(2)}) copy-start(f32[24]{0:T(128)} %copy-done.32) | copy-start | bytes 292
  410.9 23.4 %copy-start.9 = (f32[6,24,256]{2,1,0:T(8,128)S(1)}, f32[6,24,256]{2,1,0:T(8,128)}, u32[]{:S(2)}) copy-start(f32[6,24,256]{2,1,0:T(8,128)} %get-tuple-element.772) | copy-start | bytes 442372
  410.9 24.2 %copy-start.3 = (bf16[6,256,256]{1,2,0:T(8,128)(2,1)S(1)}, bf16[6,256,256]{1,2,0:T(8,128)(2,1)}, u32[]{:S(2)}) copy-start(bf16[6,256,256]{1,2,0:T(8,128)(2,1)} %get-tuple-element.771) | copy-start | bytes 2359300
  418.0 18.4 %copy-start.7 = (f32[6,256,128]{1,2,0:T(8,128)S(1)}, f32[6,256,128]{1,2,0:T(8,128)}, u32[]{:S(2)}) copy-start(f32[6,256,128]{1,2,0:T(8,128)} %copy-done.6) | copy-start | bytes 2359300
  453.6 13.1 %copy-start.23 = (f32[24]{0:T(128)S(1)}, f32[24]{0:T(128)}, u32[]{:S(2)}) copy-start(f32[24]{0:T(128)} %get-tuple-element.774) | copy-start | bytes 292
  453.6 13.7 %copy-start.35 = (f32[24]{0:T(128)S(1)}, f32[24]{0:T(128)}, u32[]{:S(2)}) copy-start(f32[24]{0:T(128)} %get-tuple-element.1787) | copy-start | bytes 292
  467.4 62.7 %copy-start.29 = (f32[24]{0:T(128)S(1)}, f32[24]{0:T(128)}, u32[]{:S(2)}) copy-start(f32[24]{0:T(128)} %get-tuple-element.775) | copy-start | bytes 292
  467.4 62.7 %copy-start.26 = (f32[24]{0:T(128)S(1)}, f32[24]{0:T(128)}, u32[]{:S(2)}) copy-start(f32[24]{0:T(128)} %get-tuple-element.776) | copy-start | bytes 292
  (70 other events, 333.1 us)
Sparse Core Ops, SparseCore 0:
  10.8 134.8 all-gather.2
where the time goes:
time: 607 us; the launch traced here: 601 us
  local copies, waits for them, and re-layouts  158 us (26%)
  matrix products  151 us (25%)
  other arithmetic  115 us (19%)
  waiting for transfers between devices  86.9 us (14%)
  blocking collectives  67.2 us (11%)
  between operations  16.4 us (3%)
    all_gather x1, waiting for transfers between devices, shards(): gathered = lax.all_gather(old_states, 'stream', axis=0, tiled=True)  83.2 us
    dot_general x18, matrix products, one_group(): jnp.einsum('hij,jhp->ihp', mixing, inputs_q, preferred_element_type=jnp.f...  81.8 us
    psum x1, blocking collectives, shards(): lax.psum((rates_first + rates_second, bias_first + bias_second, skip_tota...  64.5 us
    another operation x80, other arithmetic  52.5 us
    dot_general x24, matrix products, one_group(): jnp.einsum('in,hpn->ihp', c_part.astype(jnp.float32), starts_q, precision...  43.1 us
    unnamed x56, local copies, waits for them, and re-layouts  35.7 us
    squeeze x30, local copies, waits for them, and re-layouts, outputs(): lax.scan(per_group, 0, (inputs_c, maps_c, logits_c, flags_c, starts_c))  22.8 us
    dot_general x3, matrix products, group_states(): jnp.einsum('cjhp,chjn->chpn', inputs_c, b_weighted, preferred_element_typ...  21.9 us
  transfers between devices with their start and end apart: 3, of which 3 were waited for; matrix products, arithmetic and copies ran while one was open for 9% of the time, Pallas kernels for 0%

commit v1 on v0

--- a/solution.py
+++ b/solution.py
@@ -4,6 +4,11 @@
 from jax.sharding import PartitionSpec as P
 
 GROUP = 256
+
+
+def one_after_other(value, one, other):
+    inner = lax.psum(value, one)
+    return lax.psum(inner, other)
 
 
 def shifted_2(shard, axis, by):
@@ -151,8 +156,8 @@
     in_second, maps_second, logits_second, rates_second, bias_second = pull_states(
         (grad_states, grad_decays)
     )
-    rates_total, bias_total, skip_sum = lax.psum(
-        (rates_first + rates_second, bias_first + bias_second, skip_total), ("stream", "seq")
+    rates_total, bias_total, skip_sum = one_after_other(
+        (rates_first + rates_second, bias_first + bias_second, skip_total), "seq", "stream"
     )
     grad_logits = (logits_first + logits_second).transpose(1, 0, 2).reshape(1, head_count, length)
     return (

time: 607 us -> 721 us (1.19)
  the two profiles are of different devices: /device:TPU:1 before, /device:TPU:0 now
where the time goes in v1:
time: 721 us; the launch traced here: 716 us
  blocking collectives  182 us (25%)
  local copies, waits for them, and re-layouts  158 us (22%)
  matrix products  151 us (21%)
  other arithmetic  115 us (16%)
  waiting for transfers between devices  86.2 us (12%)
  between operations  16.4 us (2%)
    psum x1, blocking collectives, one_after_other(): return lax.psum(inner, other)  177 us
    all_gather x1, waiting for transfers between devices, shards(): gathered = lax.all_gather(old_states, 'stream', axis=0, tiled=True)  82.6 us
    dot_general x18, matrix products, one_group(): jnp.einsum('hij,jhp->ihp', mixing, inputs_q, preferred_element_type=jnp.f...  81.8 us
    another operation x80, other arithmetic  52.5 us
    dot_general x24, matrix products, one_group(): jnp.einsum('in,hpn->ihp', c_part.astype(jnp.float32), starts_q, precision...  43.1 us
    unnamed x56, local copies, waits for them, and re-layouts  35.8 us
    squeeze x30, local copies, waits for them, and re-layouts, outputs(): lax.scan(per_group, 0, (inputs_c, maps_c, logits_c, flags_c, starts_c))  22.8 us
    dot_general x3, matrix products, group_states(): jnp.einsum('cjhp,chjn->chpn', inputs_c, b_weighted, preferred_element_typ...  21.9 us
  transfers between devices with their start and end apart: 3, of which 3 were waited for; matrix products, arithmetic and copies ran while one was open for 7% of the time, Pallas kernels for 0%

profile of v1, /device:TPU:0, one launch (start us, length us, event | category | flops | bytes accessed | tf_op | source)
XLA Modules:
  0.0 715.7 jit_solution(13407831844161415959)
XLA Ops:
  21.2 12.9 %reshape.634 = bf16[6,256,24,64]{3,2,1,0:T(8,128)(2,1)} reshape(bf16[1,1536,1536]{2,1,0:T(8,128)(2,1)} %param.22) | data formatting | bytes 9437184 | tf_op jit(solution)/shard_map/reshape;squeeze | solution.py:112
  34.1 10.3 %copy.231 = bf16[6,256,24,64]{1,3,2,0:T(8,128)(2,1)} copy(bf16[6,256,24,64]{3,2,1,0:T(8,128)(2,1)} %reshape.634) | data formatting | bytes 9437184
  46.2 8.0 %fusion.94 = f32[6,24,64,128]{3,2,1,0:T(8,128)} fusion(bf16[6,256,24,64]{1,3,2,0:T(8,128)(2,1)} %copy.231, f32[6,256,128]{1,2,0:T(8,128)S(1)} %copy.228, f32[6,24,256]{2,1,0:T(8,128)S(1)} %select_multiply_fusion.3), kind=kOutput, calls=%fused_computation.172 | convolution fusion | flops 613416960 | bytes 10371072 | tf_op jit(solution)/shard_map/jvp(cjhp,chjn->chpn)/dot_general | solution.py:36
  54.2 8.0 %while.108 = (s32[]{:T(128)}, f32[24,64,128]{2,1,0:T(8,128)S(1)}, f32[6,24]{1,0:T(8,128)S(1)}, f32[6,24,64,128]{3,2,1,0:T(8,128)}, s32[]{:T(128)}, /*index=5*/s32[]{:T(128)}) while((s32[]{:T(128)}, f32[24,64,128]{2,1,0:T(8,128)S(1)}, f32[6,24]{1,0:T(8,128)S(1)}, f32[6,24,64,128]{3,2,1,0:T(8,128)}, s32[]{:T(128)}, ...), condition=%wide.region_7.8_spmd.clone, body=%wide.region_6.7_spmd.clone.sunk | while | flops 589827 | bytes 2359671 | solution.py:47
  62.3 82.6 %all-gather.3.cloned.1.call-done = f32[64,12,64,128]{3,2,1,0:T(8,128)} async-done(((f32[1,12,64,128]{3,2,1,0:T(8,128)}), f32[64,12,64,128]{3,2,1,0:T(8,128)}) %all-gather.3.cloned.1.call-update) | async-done | bytes 25165840 | tf_op jit(solution)/shard_map/all_gather | solution.py:109
  156.4 17.0 %while.105 = (s32[]{:T(128)}, f32[24,64,128]{2,1,0:T(8,128)S(1)}, f32[6,24,64,128]{3,2,1,0:T(8,128)}, f32[6,24,1,1]{1,3,2,0:T(1,128)}, f32[6,24]{1,0:T(8,128)S(1)}, /*index=5*/f32[6,24,64,128]{3,2,1,0:T(8,128)}, s32[]{:T(128)}) while((s32[]{:T(128)}, f32[24,64,128]{2,1,0:T(8,128)S(1)}, f32[6,24,64,128]{3,2,1,0:T(8,128)}, ...), condition=%wide.region_9.10_spmd, body=%wide.region_8.9_spmd.sunk | while | flops 393218 | bytes 3934165 | solution.py:47
  180.5 195.7 %while.109 = (s32[]{:T(128)}, f32[24]{0:T(128)}, f32[24]{0:T(128)}, f32[24]{0:T(128)}, bf16[6,256,24,64]{1,3,2,0:T(8,128)(2,1)}, /*index=5*/bf16[6,256,256]{1,2,...) while((s32[]{:T(128)}, f32[24]{0:T(128)}, f32[24]{0:T(128)}, ...), condition=%wide.region_31.32_spmd.clone, body=%wide.region_16.31_spmd.clone.sunk | while | flops 2306163200 | bytes 22004424 | solution.py:84
  191.9 6.2 fusion.183
  224.5 6.2 fusion.183
  257.1 6.2 fusion.183
  269.1 3.9 fusion.189
  289.8 6.2 fusion.183
  322.4 6.2 fusion.183
  355.0 6.2 fusion.183
  367.0 3.9 fusion.189
  376.2 11.6 %while.110 = (s32[]{:T(128)}, f32[24,64,128]{2,1,0:T(8,128)S(1)}, f32[6,24,64,128]{3,2,1,0:T(8,128)}, f32[6,24,1,1]{1,3,2,0:T(1,128)}, s32[]{:T(128)}, /*index=5*/s32[]{:T(128)}, s32[]{:T(128)}) while((s32[]{:T(128)}, f32[24,64,128]{2,1,0:T(8,128)S(1)}, f32[6,24,64,128]{3,2,1,0:T(8,128)}, f32[6,24,1,1]{1,3,2,0:T(1,128)}, ...), condition=%wide.region_33.34_spmd.clone, body=%wide.region_32.33_spmd.clone.sunk | while | flops 589828 | bytes 2359691 | solution.py:47
  393.2 15.2 %while.106 = (s32[]{:T(128)}, f32[24,64,128]{2,1,0:T(8,128)S(1)}, bf16[6,24,64,128]{3,2,1,0:T(8,128)(2,1)S(1)}, f32[6,24]{1,0:T(8,128)S(1)}, f32[6,24,64,128]{3,...) while((s32[]{:T(128)}, f32[24,64,128]{2,1,0:T(8,128)S(1)}, ...), condition=%wide.region_36.37_spmd, body=%wide.region_34.36_spmd.sunk | while | flops 786411 | bytes 4719297 | solution.py:47
  409.9 7.1 fusion.87
  417.7 14.9 %reduce-window.130 = f32[6,24,2,128]{3,1,2,0:T(8,128)S(1)} reduce-window(f32[6,24,2,128]{3,1,2,0:T(8,128)S(1)} %copy_bitcast_fusion.5, f32[]{:T(128)} %constant.289.clone.1), window={size=1x1x1x128 pad=0_0x0_0x0_0x0_127}, to_apply=%region_40.41 | reduce-window | flops 4681728 | bytes 294916 | tf_op jit(solution)/shard_map/reduce-window.14
  435.3 6.9 bitcast_add_fusion.6
  442.2 10.4 %copy.250 = bf16[6,256,24,64]{3,2,1,0:T(8,128)(2,1)} copy(bf16[6,256,24,64]{1,3,2,0:T(8,128)(2,1)} %bitcast_add_fusion.6) | data formatting | bytes 9437184
  452.6 13.1 %reshape.633 = bf16[1,1536,1536]{2,1,0:T(8,128)(2,1)} reshape(bf16[6,256,24,64]{3,2,1,0:T(8,128)(2,1)} %copy.250) | data formatting | bytes 9437184
  466.3 62.6 %while.107 = (s32[]{:T(128)}, bf16[6,256,1536]{2,1,0:T(8,128)(2,1)}, bf16[6,256,24,64]{1,3,2,0:T(8,128)(2,1)}, bf16[6,256,256]{2,1,0:T(8,128)(2,1)}, s32[6,256]{...) while((s32[]{:T(128)}, bf16[6,256,1536]{2,1,0:T(8,128)(2,1)}, ...), condition=%wide.region_15.16_spmd.clone, body=%wide.region_10.15_spmd.clone.sunk | while | flops 833433920 | bytes 10981461 | solution.py:84
  531.5 177.4 %all-reduce.5 = (f32[24]{0:T(128)}, f32[24]{0:T(128)}, f32[24]{0:T(128)}) all-reduce(f32[24]{0:T(128)S(1)} %get-tuple-element.1201, f32[24]{0:T(128)S(1)} %get-tuple-element.1202, f32[24]{0:T(128)S(1)} %get-tuple-element.1203), channel_id=1, replica_groups=mesh['stream'=64,'seq'=2] {'stream'}, use_global_device_ids=true, to_apply=%region_44.45 | all-reduce | flops 72 | bytes 576 | tf_op jit(solution)/shard_map/psum | solution.py:11
  (718 shorter events, 308.4 us)
Async XLA Ops:
  7.2 137.7 %all-gather.3.cloned.1.call-start = ((), (), s32[]{:S(2)}) async-start(), calls=%async_computation | async-start | bytes 25559040 | tf_op jit(solution)/shard_map/all_gather | solution.py:109
  14.3 19.8 %copy-start.32 = (f32[24]{0:T(128)}, f32[24]{0:T(128)S(1)}, u32[]{:S(2)}) copy-start(f32[24]{0:T(128)S(1)} %exp.90) | copy-start | bytes 292
  16.1 29.9 %copy-start.1 = (f32[6,24,256]{2,1,0:T(8,128)}, f32[6,24,256]{2,1,0:T(8,128)S(1)}, u32[]{:S(2)}) copy-start(f32[6,24,256]{2,1,0:T(8,128)S(1)} %get-tuple-element.1741) | copy-start | bytes 442372
  19.9 26.1 %copy-start.11 = (f32[6,24,2]{1,2,0:T(2,128)}, f32[6,24,2]{1,2,0:T(2,128)S(1)}, u32[]{:S(2)}) copy-start(f32[6,24,2]{1,2,0:T(2,128)S(1)} %slice.164) | copy-start | bytes 3460
  21.2 25.0 %copy-start.6 = (f32[6,256,128]{1,2,0:T(8,128)}, f32[6,256,128]{1,2,0:T(8,128)S(1)}, u32[]{:S(2)}) copy-start(f32[6,256,128]{1,2,0:T(8,128)S(1)} %copy.228) | copy-start | bytes 2359300
  34.1 11.9 %copy-start.10 = (f32[24]{0:T(128)S(1)}, f32[24]{0:T(128)}, u32[]{:S(2)}) copy-start(f32[24]{0:T(128)} %param.26) | copy-start | bytes 292
  45.3 8.9 %copy-start.13 = (f32[6,24]{1,0:T(8,128)}, f32[6,24]{1,0:T(8,128)S(1)}, u32[]{:S(2)}) copy-start(f32[6,24]{1,0:T(8,128)S(1)} %slice_reduce_fusion.7) | copy-start | bytes 1732
  46.0 8.2 %copy-start.19 = (pred[6,256]{1,0:T(8,128)(4,1)}, pred[6,256]{1,0:T(8,128)(4,1)S(1)}, u32[]{:S(2)}) copy-start(pred[6,256]{1,0:T(8,128)(4,1)S(1)} %broadcast_compare_fusion.2) | copy-start | bytes 4612
  149.3 4.1 collective-permute-start
  269.1 8.0 %copy-start.27 = (f32[24]{0:T(128)S(1)}, f32[24]{0:T(128)}, u32[]{:S(2)}) copy-start(f32[24]{0:T(128)} %get-tuple-element.1645) | copy-start | bytes 292 | tf_op jit(solution)/shard_map/transpose(jvp())/while
  367.0 8.0 %copy-start.27 = (f32[24]{0:T(128)S(1)}, f32[24]{0:T(128)}, u32[]{:S(2)}) copy-start(f32[24]{0:T(128)} %get-tuple-element.1645) | copy-start | bytes 292 | tf_op jit(solution)/shard_map/transpose(jvp())/while
  376.2 11.6 %copy-start.34 = (f32[24]{0:T(128)S(1)}, f32[24]{0:T(128)}, u32[]{:S(2)}) copy-start(f32[24]{0:T(128)} %broadcast_multiply_fusion) | copy-start | bytes 292
  388.8 4.4 collective-permute-start.1
  393.2 15.2 %copy-start.14 = (f32[6,24]{1,0:T(8,128)S(1)}, f32[6,24]{1,0:T(8,128)}, u32[]{:S(2)}) copy-start(f32[6,24]{1,0:T(8,128)} %copy-done.13) | copy-start | bytes 1732
  393.2 15.2 %copy-start.31 = (pred[6]{0:T(512)(128)(4,1)S(1)}, pred[6]{0:T(512)(128)(4,1)}, u32[]{:S(2)}) copy-start(pred[6]{0:T(512)(128)(4,1)} %copy-done.30) | copy-start | bytes 22
  393.2 16.6 %copy-start.16 = (f32[6,24,256]{2,1,0:T(8,128)S(1)}, f32[6,24,256]{2,1,0:T(8,128)}, u32[]{:S(2)}) copy-start(f32[6,24,256]{2,1,0:T(8,128)} %copy-done.15) | copy-start | bytes 442372
  409.8 23.0 %copy-start.33 = (f32[24]{0:T(128)S(1)}, f32[24]{0:T(128)}, u32[]{:S(2)}) copy-start(f32[24]{0:T(128)} %copy-done.32) | copy-start | bytes 292
  409.8 23.4 %copy-start.9 = (f32[6,24,256]{2,1,0:T(8,128)S(1)}, f32[6,24,256]{2,1,0:T(8,128)}, u32[]{:S(2)}) copy-start(f32[6,24,256]{2,1,0:T(8,128)} %get-tuple-element.772) | copy-start | bytes 442372
  409.8 24.2 %copy-start.3 = (bf16[6,256,256]{1,2,0:T(8,128)(2,1)S(1)}, bf16[6,256,256]{1,2,0:T(8,128)(2,1)}, u32[]{:S(2)}) copy-start(bf16[6,256,256]{1,2,0:T(8,128)(2,1)} %get-tuple-element.771) | copy-start | bytes 2359300
  416.9 18.4 %copy-start.7 = (f32[6,256,128]{1,2,0:T(8,128)S(1)}, f32[6,256,128]{1,2,0:T(8,128)}, u32[]{:S(2)}) copy-start(f32[6,256,128]{1,2,0:T(8,128)} %copy-done.6) | copy-start | bytes 2359300
  452.6 13.1 %copy-start.23 = (f32[24]{0:T(128)S(1)}, f32[24]{0:T(128)}, u32[]{:S(2)}) copy-start(f32[24]{0:T(128)} %get-tuple-element.774) | copy-start | bytes 292
  452.6 13.7 %copy-start.35 = (f32[24]{0:T(128)S(1)}, f32[24]{0:T(128)}, u32[]{:S(2)}) copy-start(f32[24]{0:T(128)} %get-tuple-element.1790) | copy-start | bytes 292
  466.3 62.7 %copy-start.29 = (f32[24]{0:T(128)S(1)}, f32[24]{0:T(128)}, u32[]{:S(2)}) copy-start(f32[24]{0:T(128)} %get-tuple-element.775) | copy-start | bytes 292
  466.3 62.7 %copy-start.26 = (f32[24]{0:T(128)S(1)}, f32[24]{0:T(128)}, u32[]{:S(2)}) copy-start(f32[24]{0:T(128)} %get-tuple-element.776) | copy-start | bytes 292
  (70 other events, 333.2 us)
Sparse Core Ops, SparseCore 0:
  10.8 134.0 all-gather.2
